TPU v7x, 32 devices: a whole 2x2x4 slice. The times are simulated.
32 devices in a mesh: freq: 8 (over y, x, core), rcv: 4 (over z).
Axes of the slice: x: 2, y: 2, z: 4, core: 2. Of those that a mesh axis runs over, the one named last changes fastest.
Arguments:
- green_freq: float32 [2, 8, 2304, 2304], P(None, 'freq', 'rcv'), may hold values from -6 to 6
- data_matrix: float32 [2, 8, 2304, 2304], P(None, 'freq', 'rcv'), may hold values from -0.09375 to 0.09375
- shot_panels: float32 [2, 8, 2304, 256], P(None, 'freq', 'rcv'), may hold values from -6 to 6
- wavelet: float32 [2, 8], P(None, 'freq'), may hold values from -1.5 to 1.5
- sources: int32 [256], replicated, may hold values from 0 to 2303, as said below
- support: int32 [8, 2304], replicated, may hold values 0 or 1
- threshold: float32 [1], replicated, may hold values from 3 to 7
Outputs:
- green_next: float32 [2, 8, 2304, 2304], P(None, 'freq', 'rcv')
- residual: float32 [2, 8, 2304, 256], P(None, 'freq', 'rcv')
Inputs may be any that keep to these rules, and one draw needn't show every extreme that they name: `sources`: 256 distinct source positions. `support`: a 0/1 mask over time samples and source positions.
All inputs are finite; a program needn't handle non-finite values.
Results may differ from a plain program's by a relative error of at most 0.00013.
Values sent between devices are 32-bit elements; how exact they have to be, the bound alone decides.
A program may use at most 128 MiB of HBM per device.

v0:
```python
import math
import jax
import jax.numpy as jnp
from jax import lax
from jax.sharding import PartitionSpec as P

HIGHEST = lax.Precision.HIGHEST


def complex_product(left_pair, right_pair, pattern):
    left_real, left_imag = left_pair
    right_real, right_imag = right_pair
    real_part = jnp.einsum(pattern, left_real, right_real, precision=HIGHEST) - jnp.einsum(
        pattern, left_imag, right_imag, precision=HIGHEST
    )
    imag_part = jnp.einsum(pattern, left_real, right_imag, precision=HIGHEST) + jnp.einsum(
        pattern, left_imag, right_real, precision=HIGHEST
    )
    return (real_part, imag_part)


def conj_product(left_pair, right_pair, pattern):
    left_real, left_imag = left_pair
    right_real, right_imag = right_pair
    real_part = jnp.einsum(pattern, left_real, right_real, precision=HIGHEST) + jnp.einsum(
        pattern, left_imag, right_imag, precision=HIGHEST
    )
    imag_part = jnp.einsum(pattern, left_real, right_imag, precision=HIGHEST) - jnp.einsum(
        pattern, left_imag, right_real, precision=HIGHEST
    )
    return (real_part, imag_part)


def shrink_spectra(spectra, keep, shrink_level):
    n_freq = spectra.shape[1]
    grid = jnp.arange(n_freq, dtype=jnp.int32)
    phase = grid[:, None] * grid[None, :] % n_freq
    angle = phase.astype(jnp.float32) * (2.0 * math.pi / n_freq)
    cos_table = jnp.cos(angle)
    sin_table = jnp.sin(angle)
    pattern = "tf,f...->t..."
    time_real = jnp.einsum(pattern, cos_table, spectra[0], precision=HIGHEST) - jnp.einsum(
        pattern, sin_table, spectra[1], precision=HIGHEST
    )
    time_imag = jnp.einsum(pattern, sin_table, spectra[0], precision=HIGHEST) + jnp.einsum(
        pattern, cos_table, spectra[1], precision=HIGHEST
    )
    magnitude = jnp.sqrt(time_real * time_real + time_imag * time_imag)
    factor = (
        jnp.maximum(magnitude - shrink_level, 0.0) / jnp.maximum(magnitude, shrink_level) * keep
    )
    kept_real = factor * time_real
    kept_imag = factor * time_imag
    back_real = (
        jnp.einsum(pattern, cos_table, kept_real, precision=HIGHEST)
        + jnp.einsum(pattern, sin_table, kept_imag, precision=HIGHEST)
    ) / n_freq
    back_imag = (
        jnp.einsum(pattern, cos_table, kept_imag, precision=HIGHEST)
        - jnp.einsum(pattern, sin_table, kept_real, precision=HIGHEST)
    ) / n_freq
    return jnp.stack([back_real, back_imag])


def on_device(green_freq, data_matrix, shot_panels, wavelet, sources, support, threshold):
    data_pair = (data_matrix[0], data_matrix[1])
    picked = jnp.take(green_freq, sources, axis=3)
    wave_real = wavelet[0][:, None, None]
    wave_imag = wavelet[1][:, None, None]
    rows_here = green_freq.shape[2]
    shard_piece = lax.all_gather(picked, "rcv", axis=2, tiled=True)
    block_real = data_matrix[0]
    block_imag = data_matrix[1]
    real_part, imag_part = complex_product(
        (block_real, block_imag), (shard_piece[0], shard_piece[1]), "frk,fkc->frc"
    )
    multiple = jnp.stack([real_part, imag_part])
    resid_real = shot_panels[0] - (wave_real * picked[0] - wave_imag * picked[1] - multiple[0])
    resid_imag = shot_panels[1] - (wave_real * picked[1] + wave_imag * picked[0] - multiple[1])
    residual = jnp.stack([resid_real, resid_imag])
    local_real = wave_real * resid_real + wave_imag * resid_imag
    local_imag = wave_real * resid_imag - wave_imag * resid_real
    adj_real, adj_imag = conj_product(data_pair, (resid_real, resid_imag), "frk,frc->kfc")
    summed_terms = -jnp.stack([adj_real, adj_imag], axis=1)
    own_rows = jnp.transpose(jnp.stack([local_real, local_imag]), (2, 0, 1, 3))
    row_offset = lax.axis_index("rcv") * rows_here
    summed_terms = summed_terms + lax.dynamic_update_slice_in_dim(
        jnp.zeros_like(summed_terms), own_rows, row_offset, 0
    )
    summed_all = lax.psum(summed_terms, "rcv")
    mine = lax.dynamic_slice_in_dim(summed_all, row_offset, rows_here, 0)
    direction = jnp.transpose(mine, (1, 2, 0, 3))
    push_real, push_imag = complex_product(
        data_pair, (summed_all[:, 0], summed_all[:, 1]), "frk,kfc->frc"
    )
    pushed = jnp.stack([push_real, push_imag])
    image_real = wave_real * direction[0] - wave_imag * direction[1] - pushed[0]
    image_imag = wave_real * direction[1] + wave_imag * direction[0] - pushed[1]
    norm_dir = jnp.sum(direction * direction)
    norm_img = jnp.sum(image_real * image_real + image_imag * image_imag)
    totals = lax.psum((norm_dir, norm_img), ("freq", "rcv"))
    step_size = totals[0] / totals[1]
    updated = green_freq.at[:, :, :, sources].add(step_size * direction)
    keep_all = support.astype(jnp.float32)
    gathered = lax.all_to_all(updated, "freq", split_axis=2, concat_axis=1, tiled=True)
    shrunk = shrink_spectra(gathered, keep_all[:, None, :], threshold[0])
    green_next = lax.all_to_all(shrunk, "freq", split_axis=1, concat_axis=2, tiled=True)
    return (green_next, residual)


def solution(mesh):
    in_specs = (
        P(None, "freq", "rcv", None),
        P(None, "freq", "rcv", None),
        P(None, "freq", "rcv", None),
        P(None, "freq"),
        P(),
        P(),
        P(),
    )
    out_specs = (P(None, "freq", "rcv", None), P(None, "freq", "rcv", None))
    return jax.shard_map(
        on_device, mesh=mesh, in_specs=in_specs, out_specs=out_specs, check_vma=False
    )
```

profile of v0, /device:TPU:0, one launch (start us, length us, event | category | flops | bytes accessed | tf_op | source)
XLA Modules:
  0.0 851.4 jit_solution(611839117997585425)
XLA Ops:
  8.6 19.2 %copy.30 = f32[2,1,576,2304]{2,0,3,1:T(2,128)} copy(f32[2,1,576,2304]{3,2,1,0:T(8,128)} %param.7) | data formatting | bytes 21233664 | tf_op args[0]
  27.8 6.5 gather_fusion
  37.8 91.2 %all-gather.2.cloned.1.call-done = f32[2,1,2304,256]{3,2,1,0:T(8,128)} async-done(((f32[2,1,576,256]{3,2,1,0:T(8,128)}), f32[2,1,2304,256]{3,2,1,0:T(8,128)}) %all-gather.2.cloned.1.call-update) | async-done | bytes 4718608 | tf_op jit(solution)/shard_map/all_gather | solution.py:71
  129.0 7.5 fusion.8
  136.6 9.7 %fusion.101 = f32[576,256]{1,0:T(8,128)S(1)} fusion(f32[256,576]{0,1:T(8,128)S(1)} %fusion.8, f32[2,1,576,2304]{3,2,1,0:T(8,128)} %param.8, f32[2,1,2304,256]{3,2,1,0:T(8,128)} %all-gather.2.cloned.1.call-done, f32[2,1,576,256]{3,2,1,0:T(8,128)} %param.9, f32[2,1,576,256]{3,2,1,0:T(8,128)S(1)} %copy-done.2, f32[]{:T(128)} %bitcast.6, f32[]{:T(128)} %bitcast.3), kind=kOutput, calls=%fused_computation.76 | convolution fusion | flops 4077748224 | bytes 10617856 | tf_op jit(solution)/shard_map/frk,fkc->frc/dot_general | solution.py:16
  146.3 11.9 %fusion.6 = f32[256,2304]{0,1:T(8,128)S(1)} fusion(f32[576,256]{1,0:T(8,128)S(1)} %fusion.101, f32[2,1,576,2304]{3,2,1,0:T(8,128)} %param.8), kind=kOutput, calls=%fused_computation.9 | convolution fusion | flops 4076863488 | bytes 8257536 | tf_op jit(solution)/shard_map/frk,frc->kfc/dot_general | solution.py:25
  162.6 5.7 fusion.98
  168.3 9.6 %fusion.4 = f32[256,2304]{0,1:T(8,128)S(1)} fusion(f32[576,256]{1,0:T(8,128)S(1)} %fusion.98, f32[2,1,576,2304]{3,2,1,0:T(8,128)S(1)} %bitcast.238), kind=kOutput, calls=%fused_computation.7 | convolution fusion | flops 4076863488 | bytes 8257536 | tf_op jit(solution)/shard_map/frk,frc->kfc/dot_general | solution.py:28
  179.3 9.7 %fusion.41 = f32[2304,1,1,256]{3,0,2,1:T(8,128)S(1)} fusion(f32[256,2304]{0,1:T(8,128)S(1)} %fusion.6, f32[576,256]{1,0:T(8,128)S(1)} %fusion.98, f32[2,1,576,2304]{3,2,1,0:T(8,128)S(1)} %bitcast.238), kind=kOutput, calls=%fused_computation.44 | convolution fusion | flops 4077453312 | bytes 10616832 | tf_op jit(solution)/shard_map/frk,frc->kfc/dot_general | solution.py:25
  189.0 9.9 %fusion.38 = f32[2304,1,1,256]{3,0,2,1:T(8,128)S(1)} fusion(f32[256,2304]{0,1:T(8,128)S(1)} %fusion.4, f32[576,256]{1,0:T(8,128)S(1)} %fusion.101, f32[2,1,576,2304]{3,2,1,0:T(8,128)S(1)} %bitcast.238), kind=kOutput, calls=%fused_computation.43 | convolution fusion | flops 4077453312 | bytes 10616832 | tf_op jit(solution)/shard_map/frk,frc->kfc/dot_general | solution.py:28
  203.8 170.5 %all-reduce.3.cloned.1.call-done = f32[2304,2,1,256]{3,0,2,1:T(8,128)} async-done(((f32[2304,2,1,256]{3,0,2,1:T(8,128)}), f32[2304,2,1,256]{3,0,2,1:T(8,128)}) %all-reduce.3.cloned.1.call-update) | async-done | bytes 4718608 | tf_op jit(solution)/shard_map/psum | solution.py:90
  376.7 7.8 fusion
  384.5 7.0 fusion.2
  391.5 5.6 fusion.83
  397.2 6.3 fusion.109
  403.5 39.4 %all-reduce = (f32[]{:T(128)}, f32[]{:T(128)}) all-reduce(f32[]{:T(128)} %get-tuple-element.8, f32[]{:T(128)} %fusion.109), channel_id=1, replica_groups=mesh['freq'=8,'rcv'=4] {'freq','rcv'}, use_global_device_ids=true, to_apply=%region_2.3 | all-reduce | flops 2 | bytes 16 | tf_op jit(solution)/shard_map/psum | solution.py:101
  449.2 31.0 %scatter_fusion = f32[2,576,2304]{1,0,2:T(2,128)} fusion(f32[2,576,2304]{1,0,2:T(2,128)} %bitcast.242, s32[256]{0:T(256)S(1)} %compare_select_fusion, f32[256,2,576]{2,1,0:T(2,128)S(1)} %copy.36), kind=kCustom, calls=%fused_computation.1 | custom fusion | flops 294912 | bytes 3539968 | tf_op jit(solution)/shard_map/scatter-add | solution.py:103
  480.3 21.2 %copy.37 = f32[2,1,576,2304]{3,0,1,2:T(2,128)} copy(f32[2,1,576,2304]{2,0,3,1:T(2,128)} %bitcast.243) | data formatting | bytes 21233664 | tf_op jit(solution)/shard_map/scatter-add | solution.py:103
  501.5 5.3 all-to-all-start
  507.5 117.2 %all-to-all-done = f32[2,1,576,2304]{3,0,1,2:T(2,128)} async-done(((f32[2,1,576,2304]{3,0,1,2:T(2,128)}), f32[2,1,576,2304]{3,0,1,2:T(2,128)}, u32[]{:S(2)}, u32[]{:S(2)}) %all-to-all-start) | async-done | bytes 10616864 | tf_op jit(solution)/shard_map/all_to_all | solution.py:105
  624.7 12.6 %fusion.174 = (f32[1,1,576,2304]{3,0,1,2:T(1,128)S(1)}, f32[1,1,576,2304]{3,0,1,2:T(1,128)S(1)}) fusion(f32[2,1,576,2304]{3,0,1,2:T(2,128)} %all-to-all-done), kind=kLoop, calls=%fused_computation.145 | loop fusion | bytes 21233664 | tf_op jit(solution)/shard_map/slice | solution.py:43
  637.7 7.0 fusion.30
  644.7 7.0 fusion.28
  652.1 7.1 convolution_subtract_fusion
  659.2 7.4 convolution_add_fusion
  666.6 7.6 fusion.121
  674.3 8.0 fusion.119
  682.3 8.8 %multiply_bitcast_fusion.1 = f32[1,8,72,2304]{3,1,2,0:T(8,128)} fusion(f32[8,72,2304]{2,0,1:T(8,128)S(1)} %fusion.121, f32[8,72,2304]{2,0,1:T(8,128)S(1)} %convolution_add_fusion, f32[8,72,2304]{2,0,1:T(8,128)S(1)} %convolution_subtract_fusion, f32[8,2304]{1,0:T(8,128)S(1)} %convert_element_type.21, f32[]{:T(128)} %bitcast.234), kind=kOutput, calls=%fused_computation.28 | convolution fusion | flops 142001024 | bytes 21307396 | tf_op jit(solution)/shard_map/tf,f...->t.../dot_general | solution.py:56
  691.1 9.0 %multiply_bitcast_fusion = f32[1,8,72,2304]{3,1,2,0:T(8,128)} fusion(f32[8,72,2304]{2,0,1:T(8,128)S(1)} %fusion.119, f32[8,72,2304]{2,0,1:T(8,128)S(1)} %convolution_subtract_fusion, f32[8,72,2304]{2,0,1:T(8,128)S(1)} %convolution_add_fusion, f32[8,2304]{1,0:T(8,128)S(1)} %convert_element_type.21, f32[]{:T(128)} %bitcast.235), kind=kOutput, calls=%fused_computation.27 | convolution fusion | flops 142001024 | bytes 21307396 | tf_op jit(solution)/shard_map/tf,f...->t.../dot_general | solution.py:60
  704.9 7.4 copy.44
  718.5 116.8 %all-to-all-done.1 = f32[2,8,72,2304]{3,2,0,1:T(8,128)} async-done(((f32[2,8,72,2304]{3,2,0,1:T(8,128)}), f32[2,8,72,2304]{3,2,0,1:T(8,128)}, u32[]{:S(2)}, u32[]{:S(2)}) %all-to-all-start.1) | async-done | bytes 10616864 | tf_op jit(solution)/shard_map/all_to_all | solution.py:107
  835.3 9.0 %copy.45 = f32[2,8,72,2304]{3,2,1,0:T(8,128)} copy(f32[2,8,72,2304]{3,2,0,1:T(8,128)} %all-to-all-done.1) | data formatting | bytes 21233664 | tf_op jit(solution)/shard_map/all_to_all | solution.py:107
  (54 shorter events, 34.6 us)
Async XLA Ops:
  7.2 121.9 %all-gather.2.cloned.1.call-start = ((), (), s32[]{:S(2)}) async-start(), calls=%async_computation.2 | async-start | bytes 5898240 | tf_op jit(solution)/shard_map/all_gather | solution.py:71
  27.8 9.3 %copy-start.5 = (f32[2,1]{0,1:T(1,128)S(1)}, f32[2,1]{0,1:T(1,128)}, u32[]{:S(2)}) copy-start(f32[2,1]{0,1:T(1,128)} %param.10) | copy-start | bytes 28
  36.7 99.8 %copy-start.2 = (f32[2,1,576,256]{3,2,1,0:T(8,128)S(1)}, f32[2,1,576,256]{3,2,1,0:T(8,128)}, u32[]{:S(2)}) copy-start(f32[2,1,576,256]{3,2,1,0:T(8,128)} %bitcast_select_fusion) | copy-start | bytes 3538948
  36.8 337.6 %all-reduce.3.cloned.1.call-start = ((), (), s32[]{:S(2)}) async-start(), calls=%async_computation.3 | async-start | bytes 9437184 | tf_op jit(solution)/shard_map/psum | solution.py:90
  129.0 29.2 %slice-start = ((s8[10616832]{0:T(1024)(128)(4,1)}), s8[4194304]{0:T(1024)(128)(4,1)S(1)}, s32[]{:S(2)}) async-start(s8[10616832]{0:T(1024)(128)(4,1)} %bitcast.237), calls=%async_computation.4 | async-start | bytes 8388608
  129.0 29.2 %slice-start.6 = ((s8[4718592]{0:T(1024)(128)(4,1)}), s8[4194304]{0:T(1024)(128)(4,1)S(1)}, s32[]{:S(2)}) async-start(s8[4718592]{0:T(1024)(128)(4,1)} %bitcast.248), calls=%async_computation.10 | async-start | bytes 8388608
  136.5 21.7 %slice-start.1 = ((s8[10616832]{0:T(1024)(128)(4,1)}), s8[4194304]{0:T(1024)(128)(4,1)S(1)}, s32[]{:S(2)}) async-start(s8[10616832]{0:T(1024)(128)(4,1)} %bitcast.237), calls=%async_computation.5 | async-start | bytes 8388608
  136.5 21.7 %slice-start.2 = ((s8[10616832]{0:T(1024)(128)(4,1)}), s8[2228224]{0:T(1024)(128)(4,1)S(1)}, s32[]{:S(2)}) async-start(s8[10616832]{0:T(1024)(128)(4,1)} %bitcast.237), calls=%async_computation.6 | async-start | bytes 4456448
  136.5 21.7 %slice-start.7 = ((s8[4718592]{0:T(1024)(128)(4,1)}), s8[524288]{0:T(1024)(128)(4,1)S(1)}, s32[]{:S(2)}) async-start(s8[4718592]{0:T(1024)(128)(4,1)} %bitcast.248), calls=%async_computation.11 | async-start | bytes 1048576
  158.2 4.4 copy-start.3
  203.8 187.7 %slice-start.3 = ((s8[10616832]{0:T(1024)(128)(4,1)}), s8[2228224]{0:T(1024)(128)(4,1)S(1)}, s32[]{:S(2)}) async-start(s8[10616832]{0:T(1024)(128)(4,1)} %bitcast.239), calls=%async_computation.7 | async-start | bytes 4456448
  374.4 10.2 %copy-start = (f32[2304,2,1,256]{3,0,2,1:T(8,128)S(1)}, f32[2304,2,1,256]{3,0,2,1:T(8,128)}, u32[]{:S(2)}) copy-start(f32[2304,2,1,256]{3,0,2,1:T(8,128)} %all-reduce.3.cloned.1.call-done) | copy-start | bytes 14155780
  376.7 20.5 %copy-start.1 = (f32[2,1,576,256]{3,2,1,0:T(8,128)}, f32[2,1,576,256]{3,2,1,0:T(8,128)S(1)}, u32[]{:S(2)}) copy-start(f32[2,1,576,256]{3,2,1,0:T(8,128)S(1)} %get-tuple-element.9) | copy-start | bytes 3538948
  376.7 14.8 %slice-start.4 = ((s8[10616832]{0:T(1024)(128)(4,1)}), s8[4194304]{0:T(1024)(128)(4,1)S(1)}, s32[]{:S(2)}) async-start(s8[10616832]{0:T(1024)(128)(4,1)} %bitcast.239), calls=%async_computation.8 | async-start | bytes 8388608
  384.5 7.0 slice-start.5
  501.5 5.3 copy-start.4
  501.5 123.2 %all-to-all-start = ((f32[2,1,576,2304]{3,0,1,2:T(2,128)}), f32[2,1,576,2304]{3,0,1,2:T(2,128)}, u32[]{:S(2)}, u32[]{:S(2)}) async-start(f32[2,1,576,2304]{3,0,1,2:T(2,128)} %copy.37), calls=%async_computation | async-start | bytes 21233664 | tf_op jit(solution)/shard_map/all_to_all | solution.py:105
  712.2 123.1 %all-to-all-start.1 = ((f32[2,8,72,2304]{3,2,0,1:T(8,128)}), f32[2,8,72,2304]{3,2,0,1:T(8,128)}, u32[]{:S(2)}, u32[]{:S(2)}) async-start(f32[2,8,72,2304]{3,2,0,1:T(8,128)} %copy.44), calls=%async_computation.1 | async-start | bytes 21233664 | tf_op jit(solution)/shard_map/all_to_all | solution.py:107
Sparse Core Ops, SparseCore 0:
  36.9 92.0 all-gather.1
  203.9 170.3 all-reduce.2
where the time goes:
time: 856 us; the launch traced here: 851 us
  waiting for transfers between devices  496 us (58%)
  matrix products  157 us (18%)
  local copies, waits for them, and re-layouts  81.3 us (9%)
  other arithmetic  50.4 us (6%)
  blocking collectives  39.4 us (5%)
  between operations  16.6 us (2%)
  starting transfers between devices  10.8 us (1%)
    psum x1, waiting for transfers between devices, on_device(): summed_all = lax.psum(summed_terms, 'rcv')  171 us
    all_to_all x1, waiting for transfers between devices, on_device(): lax.all_to_all(updated, 'freq', split_axis=2, concat_axis=1, tiled=True)  117 us
    all_to_all x1, waiting for transfers between devices, on_device(): lax.all_to_all(shrunk, 'freq', split_axis=1, concat_axis=2, tiled=True)  117 us
    all_gather x1, waiting for transfers between devices, on_device(): shard_piece = lax.all_gather(picked, 'rcv', axis=2, tiled=True)  91.2 us
    psum x1, blocking collectives, on_device(): totals = lax.psum((norm_dir, norm_img), ('freq', 'rcv'))  39.4 us
    scatter-add x1, other arithmetic, on_device(): updated = green_freq.at[:, :, :, sources].add(step_size * direction)  31 us
    scatter-add x1, local copies, waits for them, and re-layouts, on_device(): updated = green_freq.at[:, :, :, sources].add(step_size * direction)  21.2 us
    unnamed x31, local copies, waits for them, and re-layouts  20 us
  transfers between devices with their start and end apart: 4, of which 4 were waited for; matrix products, arithmetic and copies ran while one was open for 0% of the time, Pallas kernels for 0%

commit v1 on v0

--- a/solution.py
+++ b/solution.py
@@ -87,7 +87,11 @@
     summed_terms = summed_terms + lax.dynamic_update_slice_in_dim(
         jnp.zeros_like(summed_terms), own_rows, row_offset, 0
     )
-    summed_all = lax.psum(summed_terms, "rcv")
+    summed_all = summed_terms
+    for hop in (1, 2):
+        summed_all = summed_all + lax.ppermute(
+            summed_all, "rcv", [(dev, dev ^ hop) for dev in range(4)]
+        )
     mine = lax.dynamic_slice_in_dim(summed_all, row_offset, rows_here, 0)
     direction = jnp.transpose(mine, (1, 2, 0, 3))
     push_real, push_imag = complex_product(

time: 856 us -> 986 us (1.15)
  waiting for transfers between devices: 496 us -> 633 us
    ppermute x0 -> x2, waiting for transfers between devices: none -> 307 us  [on_device(): lax.ppermute(summed_all, 'rcv', [(dev, dev ^ hop) for dev in range(4)])]
    psum x1 -> x0, waiting for transfers between devices: 171 us -> none  [on_device(): summed_all = lax.psum(summed_terms, 'rcv')]
    unnamed x31 -> x21, local copies, waits for them, and re-layouts: 20 us -> 20 us
  transfers between devices with their start and end apart: 4 -> 5, of which waited for: 4 -> 5; matrix products, arithmetic and copies ran while one was open for 0% -> 0% of each run, Pallas kernels for 0% -> 0%
where the time goes in v1:
time: 986 us; the launch traced here: 978 us
  waiting for transfers between devices  633 us (64%)
  matrix products  153 us (16%)
  local copies, waits for them, and re-layouts  81.1 us (8%)
  other arithmetic  44.6 us (5%)
  blocking collectives  38 us (4%)
  between operations  16.6 us (2%)
  starting transfers between devices  11.4 us (1%)
    ppermute x2, waiting for transfers between devices, on_device(): lax.ppermute(summed_all, 'rcv', [(dev, dev ^ hop) for dev in range(4)])  307 us
    all_to_all x1, waiting for transfers between devices, on_device(): lax.all_to_all(updated, 'freq', split_axis=2, concat_axis=1, tiled=True)  117 us
    all_to_all x1, waiting for transfers between devices, on_device(): lax.all_to_all(shrunk, 'freq', split_axis=1, concat_axis=2, tiled=True)  117 us
    all_gather x1, waiting for transfers between devices, on_device(): shard_piece = lax.all_gather(picked, 'rcv', axis=2, tiled=True)  91.6 us
    psum x1, blocking collectives, on_device(): totals = lax.psum((norm_dir, norm_img), ('freq', 'rcv'))  38 us
    scatter-add x1, other arithmetic, on_device(): updated = green_freq.at[:, :, :, sources].add(step_size * direction)  31 us
    scatter-add x1, local copies, waits for them, and re-layouts, on_device(): updated = green_freq.at[:, :, :, sources].add(step_size * direction)  21.2 us
    unnamed x21, local copies, waits for them, and re-layouts  20 us
  transfers between devices with their start and end apart: 5, of which 5 were waited for; matrix products, arithmetic and copies ran while one was open for 0% of the time, Pallas kernels for 0%

profile of v1, /device:TPU:0, one launch (start us, length us, event | category | flops | bytes accessed | tf_op | source)
XLA Modules:
  0.0 978.2 jit_solution(17173900649147646454)
XLA Ops:
  8.6 19.2 %copy.30 = f32[2,1,576,2304]{2,0,3,1:T(2,128)} copy(f32[2,1,576,2304]{3,2,1,0:T(8,128)} %param.7) | data formatting | bytes 21233664 | tf_op args[0]
  27.8 6.5 gather_fusion
  37.4 91.6 %all-gather.2.cloned.1.call-done = f32[2,1,2304,256]{3,2,1,0:T(8,128)} async-done(((f32[2,1,576,256]{3,2,1,0:T(8,128)}), f32[2,1,2304,256]{3,2,1,0:T(8,128)}) %all-gather.2.cloned.1.call-update) | async-done | bytes 4718608 | tf_op jit(solution)/shard_map/all_gather | solution.py:71
  129.0 7.5 fusion.8
  136.6 9.4 fusion.101
  146.0 11.8 %fusion.6 = f32[256,2304]{0,1:T(8,128)S(1)} fusion(f32[576,256]{1,0:T(8,128)S(1)} %fusion.101, f32[2,1,576,2304]{3,2,1,0:T(8,128)} %param.8), kind=kOutput, calls=%fused_computation.9 | convolution fusion | flops 4076863488 | bytes 8257536 | tf_op jit(solution)/shard_map/frk,frc->kfc/dot_general | solution.py:25
  162.3 5.8 fusion.98
  168.1 10.4 %fusion.4 = f32[256,2304]{0,1:T(8,128)S(1)} fusion(f32[576,256]{1,0:T(8,128)S(1)} %fusion.98, f32[2,1,576,2304]{3,2,1,0:T(8,128)S(1)} %bitcast.238), kind=kOutput, calls=%fused_computation.7 | convolution fusion | flops 4076863488 | bytes 8257536 | tf_op jit(solution)/shard_map/frk,frc->kfc/dot_general | solution.py:28
  179.9 10.5 %fusion.41 = f32[2304,1,1,256]{3,0,2,1:T(8,128)S(1)} fusion(f32[256,2304]{0,1:T(8,128)S(1)} %fusion.6, f32[576,256]{1,0:T(8,128)S(1)} %fusion.98, f32[2,1,576,2304]{3,2,1,0:T(8,128)S(1)} %bitcast.238), kind=kOutput, calls=%fused_computation.44 | convolution fusion | flops 4077453312 | bytes 10616832 | tf_op jit(solution)/shard_map/frk,frc->kfc/dot_general | solution.py:25
  190.4 10.7 %fusion.38 = f32[2304,1,1,256]{3,0,2,1:T(8,128)S(1)} fusion(f32[256,2304]{0,1:T(8,128)S(1)} %fusion.4, f32[576,256]{1,0:T(8,128)S(1)} %fusion.101, f32[2,1,576,2304]{3,2,1,0:T(8,128)S(1)} %bitcast.238), kind=kOutput, calls=%fused_computation.43 | convolution fusion | flops 4077453312 | bytes 10616832 | tf_op jit(solution)/shard_map/frk,frc->kfc/dot_general | solution.py:28
  201.7 103.5 %collective-permute-done = f32[2304,2,1,256]{3,0,2,1:T(8,128)S(1)} collective-permute-done((f32[2304,2,1,256]{3,0,2,1:T(8,128)S(1)}, f32[2304,2,1,256]{3,0,2,1:T(8,128)S(1)}, u32[]{:S(2)}, u32[]{:S(2)}) %collective-permute-start) | collective-permute-done | bytes 4718624 | tf_op jit(solution)/shard_map/ppermute | solution.py:92
  306.6 203.9 %collective-permute-done.1 = f32[2304,2,1,256]{3,0,2,1:T(8,128)S(1)} collective-permute-done((f32[2304,2,1,256]{3,0,2,1:T(8,128)S(1)}, f32[2304,2,1,256]{3,0,2,1:T(8,128)S(1)}, u32[]{:S(2)}, u32[]{:S(2)}) %collective-permute-start.1) | collective-permute-done | bytes 4718624 | tf_op jit(solution)/shard_map/ppermute | solution.py:92
  521.0 5.7 fusion.83
  526.7 6.4 fusion.109
  533.1 38.0 %all-reduce = (f32[]{:T(128)}, f32[]{:T(128)}) all-reduce(f32[]{:T(128)} %get-tuple-element.8, f32[]{:T(128)} %fusion.109), channel_id=1, replica_groups=mesh['freq'=8,'rcv'=4] {'freq','rcv'}, use_global_device_ids=true, to_apply=%region_1.2 | all-reduce | flops 2 | bytes 16 | tf_op jit(solution)/shard_map/psum | solution.py:105
  576.2 31.0 %scatter_fusion = f32[2,576,2304]{1,0,2:T(2,128)} fusion(f32[2,576,2304]{1,0,2:T(2,128)} %bitcast.240, s32[256]{0:T(256)S(1)} %compare_select_fusion, f32[256,2,576]{2,1,0:T(2,128)S(1)} %copy.36), kind=kCustom, calls=%fused_computation.1 | custom fusion | flops 294912 | bytes 3539968 | tf_op jit(solution)/shard_map/scatter-add | solution.py:107
  607.2 21.2 %copy.37 = f32[2,1,576,2304]{3,0,1,2:T(2,128)} copy(f32[2,1,576,2304]{2,0,3,1:T(2,128)} %bitcast.241) | data formatting | bytes 21233664 | tf_op jit(solution)/shard_map/scatter-add | solution.py:107
  628.5 5.3 all-to-all-start
  634.4 117.2 %all-to-all-done = f32[2,1,576,2304]{3,0,1,2:T(2,128)} async-done(((f32[2,1,576,2304]{3,0,1,2:T(2,128)}), f32[2,1,576,2304]{3,0,1,2:T(2,128)}, u32[]{:S(2)}, u32[]{:S(2)}) %all-to-all-start) | async-done | bytes 10616864 | tf_op jit(solution)/shard_map/all_to_all | solution.py:109
  751.7 12.4 %fusion.174 = (f32[1,1,576,2304]{3,0,1,2:T(1,128)S(1)}, f32[1,1,576,2304]{3,0,1,2:T(1,128)S(1)}) fusion(f32[2,1,576,2304]{3,0,1,2:T(2,128)} %all-to-all-done), kind=kLoop, calls=%fused_computation.145 | loop fusion | bytes 21233664 | tf_op jit(solution)/shard_map/slice | solution.py:43
  764.5 7.0 fusion.30
  771.5 7.0 fusion.28
  778.9 7.1 convolution_subtract_fusion
  786.0 7.4 convolution_add_fusion
  793.4 7.6 fusion.121
  801.1 8.0 fusion.119
  809.1 8.8 multiply_bitcast_fusion.1
  817.9 9.0 multiply_bitcast_fusion
  831.7 7.4 copy.44
  839.0 5.2 all-to-all-start.1
  845.3 116.8 %all-to-all-done.1 = f32[2,8,72,2304]{3,2,0,1:T(8,128)} async-done(((f32[2,8,72,2304]{3,2,0,1:T(8,128)}), f32[2,8,72,2304]{3,2,0,1:T(8,128)}, u32[]{:S(2)}, u32[]{:S(2)}) %all-to-all-start.1) | async-done | bytes 10616864 | tf_op jit(solution)/shard_map/all_to_all | solution.py:111
  962.1 9.0 copy.45
  (46 shorter events, 33.1 us)
Async XLA Ops:
  7.2 121.9 %all-gather.2.cloned.1.call-start = ((), (), s32[]{:S(2)}) async-start(), calls=%async_computation.2 | async-start | bytes 5898240 | tf_op jit(solution)/shard_map/all_gather | solution.py:71
  27.8 8.9 copy-start.3
  36.7 99.8 %copy-start = (f32[2,1,576,256]{3,2,1,0:T(8,128)S(1)}, f32[2,1,576,256]{3,2,1,0:T(8,128)}, u32[]{:S(2)}) copy-start(f32[2,1,576,256]{3,2,1,0:T(8,128)} %bitcast_select_fusion) | copy-start | bytes 3538948
  36.7 99.8 %copy-start.1 = (f32[2,1,576,256]{3,2,1,0:T(8,128)S(1)}, f32[2,1,576,256]{3,2,1,0:T(8,128)}, u32[]{:S(2)}) copy-start(f32[2,1,576,256]{3,2,1,0:T(8,128)} %param.9) | copy-start | bytes 3538948
  129.0 28.8 %slice-start = ((s8[10616832]{0:T(1024)(128)(4,1)}), s8[4194304]{0:T(1024)(128)(4,1)S(1)}, s32[]{:S(2)}) async-start(s8[10616832]{0:T(1024)(128)(4,1)} %bitcast.237), calls=%async_computation.3 | async-start | bytes 8388608
  129.0 28.8 %slice-start.3 = ((s8[4718592]{0:T(1024)(128)(4,1)}), s8[4194304]{0:T(1024)(128)(4,1)S(1)}, s32[]{:S(2)}) async-start(s8[4718592]{0:T(1024)(128)(4,1)} %bitcast.246), calls=%async_computation.6 | async-start | bytes 8388608
  136.5 21.3 %slice-start.1 = ((s8[10616832]{0:T(1024)(128)(4,1)}), s8[4194304]{0:T(1024)(128)(4,1)S(1)}, s32[]{:S(2)}) async-start(s8[10616832]{0:T(1024)(128)(4,1)} %bitcast.237), calls=%async_computation.4 | async-start | bytes 8388608
  136.5 21.3 %slice-start.2 = ((s8[10616832]{0:T(1024)(128)(4,1)}), s8[2228224]{0:T(1024)(128)(4,1)S(1)}, s32[]{:S(2)}) async-start(s8[10616832]{0:T(1024)(128)(4,1)} %bitcast.237), calls=%async_computation.5 | async-start | bytes 4456448
  136.6 21.3 %slice-start.4 = ((s8[4718592]{0:T(1024)(128)(4,1)}), s8[524288]{0:T(1024)(128)(4,1)S(1)}, s32[]{:S(2)}) async-start(s8[4718592]{0:T(1024)(128)(4,1)} %bitcast.246), calls=%async_computation.7 | async-start | bytes 1048576
  201.6 103.6 %collective-permute-start = (f32[2304,2,1,256]{3,0,2,1:T(8,128)S(1)}, f32[2304,2,1,256]{3,0,2,1:T(8,128)S(1)}, u32[]{:S(2)}, u32[]{:S(2)}) collective-permute-start(f32[2304,2,1,256]{3,0,2,1:T(8,128)S(1)} %fusion.108), channel_id=1, source_target_pairs={{0,1},{1,0},{2,3},{3,2},{4,5},{5,4},{6,7},{7,6},{8,9},{9,8},{10,11... | collective-permute-start | bytes 14155784 | tf_op jit(solution)/shard_map/ppermute | solution.py:92
  305.8 204.7 %collective-permute-start.1 = (f32[2304,2,1,256]{3,0,2,1:T(8,128)S(1)}, f32[2304,2,1,256]{3,0,2,1:T(8,128)S(1)}, u32[]{:S(2)}, u32[]{:S(2)}) collective-permute-start(f32[2304,2,1,256]{3,0,2,1:T(8,128)S(1)} %add.117), channel_id=1, source_target_pairs={{0,2},{1,3},{2,0},{3,1},{4,6},{5,7},{6,4},{7,5},{8,10},{9,11},{10,... | collective-permute-start | bytes 14155784 | tf_op jit(solution)/shard_map/ppermute | solution.py:92
  628.4 5.3 copy-start.2
  628.5 123.2 %all-to-all-start = ((f32[2,1,576,2304]{3,0,1,2:T(2,128)}), f32[2,1,576,2304]{3,0,1,2:T(2,128)}, u32[]{:S(2)}, u32[]{:S(2)}) async-start(f32[2,1,576,2304]{3,0,1,2:T(2,128)} %copy.37), calls=%async_computation | async-start | bytes 21233664 | tf_op jit(solution)/shard_map/all_to_all | solution.py:109
  839.0 123.1 %all-to-all-start.1 = ((f32[2,8,72,2304]{3,2,0,1:T(8,128)}), f32[2,8,72,2304]{3,2,0,1:T(8,128)}, u32[]{:S(2)}, u32[]{:S(2)}) async-start(f32[2,8,72,2304]{3,2,0,1:T(8,128)} %copy.44), calls=%async_computation.1 | async-start | bytes 21233664 | tf_op jit(solution)/shard_map/all_to_all | solution.py:111
Sparse Core Ops, SparseCore 0:
  36.9 92.0 all-gather.1
